TPU v7x, 32 devices: a whole 2x2x4 slice. The times are simulated.
32 devices in a mesh: ctx: 8 (over y, x, core), qry: 4 (over z).
Axes of the slice: x: 2, y: 2, z: 4, core: 2. Of those that a mesh axis runs over, the one named last changes fastest.
Arguments:
- idx_query: bfloat16 [32, 8192], P('ctx', 'qry'), may hold values from -200 to 200
- idx_weight: bfloat16 [32, 64], P('ctx', 'qry'), may hold values from -3 to 3
- idx_keys: bfloat16 [16384, 128], P('ctx'), may hold values from -6 to 6
- q_latent: bfloat16 [32, 73728], P(('ctx', 'qry')), may hold values from -400 to 400
- latent_cache: bfloat16 [16384, 576], P('ctx'), may hold values from -20 to 20
- page_ids: int32 [32, 32], P(('ctx', 'qry')), may hold values from 0 to 255, as said below
Outputs:
- index_logp: float32 [32, 16384], P(('ctx', 'qry'))
- latent_out: bfloat16 [32, 65536], P(('ctx', 'qry'))
Inputs may be any that keep to these rules, and one draw needn't show every extreme that they name: `page_ids`: each row names 32 distinct pages, and no page id appears twice in the 1 row of one device (aligned blocks of 1 row). Page p holds tokens p * 64 to p * 64 + 63; ctx index j holds pages j * 32 to (j + 1) * 32 - 1. Of the 32 ids in the rows of one device, at most 8 lie on one ctx index, and in every such block some ctx index holds exactly 8.
All inputs are finite; a program needn't handle non-finite values.
Results may differ from a plain program's by a relative error of at most 0.013.
Values may be sent and summed in bfloat16 or wider, within the bound.
A program may use at most 64 MiB of HBM per device.

v0:
```python
import jax
import jax.numpy as jnp
from jax import lax
from jax.sharding import PartitionSpec as P

H_IDX = 64
D_IDX = 128
H = 128
D_LAT = 512
D_ROPE = 64
QK_NOPE = 128
PAGE = 64
TOPP = 32


def slot_ranks(requests, pages_dev):
    owner_shard = requests // pages_dev
    positions = jnp.arange(requests.shape[-1])
    earlier = positions[None, :] < positions[:, None]
    same_owner = owner_shard[..., :, None] == owner_shard[..., None, :]
    slot_rank = jnp.sum((same_owner & earlier).astype(jnp.int32), axis=-1)
    return (owner_shard, slot_rank)


def per_device(idx_query, idx_weight, idx_keys, q_latent, latent_cache, page_ids):
    shard_count = lax.axis_size("ctx")
    group_count = lax.axis_size("qry")
    ctx_index = lax.axis_index("ctx")
    rows_dev = q_latent.shape[0]
    ctx_dev = idx_keys.shape[0]
    latent_width = latent_cache.shape[1]
    pages_dev = ctx_dev // PAGE
    capacity = max(2, 2 * rows_dev * TOPP // shard_count)
    group_size = shard_count * rows_dev
    local_query = idx_query.reshape(group_count, rows_dev, idx_query.shape[1])
    local_weight = idx_weight.reshape(group_count, rows_dev, idx_weight.shape[1])
    every_query, every_weight = (
        lax.all_gather(local_query, "ctx", axis=0, tiled=True),
        lax.all_gather(local_weight, "ctx", axis=0, tiled=True),
    )
    group_query, group_weight = (
        lax.all_to_all(
            every_query.reshape(shard_count, group_count, rows_dev, idx_query.shape[1]),
            "qry",
            split_axis=1,
            concat_axis=3,
            tiled=True,
        ),
        lax.all_to_all(
            every_weight.reshape(shard_count, group_count, rows_dev, idx_weight.shape[1]),
            "qry",
            split_axis=1,
            concat_axis=3,
            tiled=True,
        ),
    )
    flat_query = group_query.reshape(group_size * H_IDX, D_IDX)
    head_weights = group_weight.reshape(group_size, H_IDX).astype(jnp.float32)
    block_width = min(512, ctx_dev)

    def score_block(step, table):
        key_block = lax.dynamic_slice_in_dim(idx_keys, step * block_width, block_width, 0)
        head_dots = lax.dot_general(
            flat_query, key_block, (((1,), (1,)), ((), ())), preferred_element_type=jnp.float32
        )
        active = jnp.maximum(head_dots, 0.0).reshape(group_size, H_IDX, block_width)
        summed = jnp.sum(active * head_weights[:, :, None], axis=1)
        return lax.dynamic_update_slice_in_dim(table, summed, step * block_width, 1)

    scores = lax.fori_loop(
        0, ctx_dev // block_width, score_block, jnp.zeros((group_size, ctx_dev), jnp.float32)
    )
    log_length = jnp.log(jnp.float32(ctx_dev * shard_count))
    score_table = lax.all_to_all(
        scores.astype(jnp.bfloat16), "ctx", split_axis=0, concat_axis=1, tiled=True
    ).astype(scores.dtype)
    row_max = jnp.max(score_table, axis=1, keepdims=True)
    row_total = jnp.sum(jnp.exp(score_table - row_max), axis=1, keepdims=True)
    index_logp = score_table - (row_max + jnp.log(row_total)) + log_length
    group_ids = lax.all_gather(page_ids, "ctx", axis=0, tiled=True)
    owner_shard, slot_rank = slot_ranks(group_ids, pages_dev)
    local_page = group_ids % pages_dev
    chosen = (owner_shard == ctx_index)[:, None, :] & (
        slot_rank[:, None, :] == jnp.arange(capacity)[None, :, None]
    )
    slot_page = jnp.sum(jnp.where(chosen, local_page[:, None, :], 0), axis=2)
    page_store = latent_cache.reshape(pages_dev, PAGE, latent_width)
    slot_keys = page_store[slot_page]
    logit_scale = (QK_NOPE + D_ROPE) ** (-0.5)
    arrived = lax.all_to_all(slot_keys, "ctx", split_axis=0, concat_axis=0, tiled=True)
    own_owner, own_rank = slot_ranks(page_ids.reshape(rows_dev * TOPP), pages_dev)
    slot_index = own_owner * capacity + own_rank
    key_rows = arrived.reshape(shard_count * capacity, PAGE, latent_width)[slot_index]
    key_rows = key_rows.reshape(rows_dev, TOPP * PAGE, latent_width)
    query_rows = q_latent.reshape(rows_dev, H, latent_width)
    logits = (
        jnp.einsum("qhd,qkd->qhk", query_rows, key_rows, preferred_element_type=jnp.float32)
        * logit_scale
    )
    logit_max = jnp.max(logits, axis=2, keepdims=True)
    expo = jnp.exp(logits - logit_max)
    att_weights = (expo / jnp.sum(expo, axis=2, keepdims=True)).astype(jnp.bfloat16)
    mixed_rows = jnp.einsum(
        "qhk,qkd->qhd", att_weights, key_rows[:, :, :D_LAT], preferred_element_type=jnp.float32
    )
    latent_out = mixed_rows.astype(jnp.bfloat16).reshape(rows_dev, H * D_LAT)
    return (index_logp, latent_out)


def solution(mesh):
    in_specs = (
        P("ctx", "qry"),
        P("ctx", "qry"),
        P("ctx", None),
        P(("ctx", "qry"), None),
        P("ctx", None),
        P(("ctx", "qry"), None),
    )
    out_specs = (P(("ctx", "qry"), None), P(("ctx", "qry"), None))
    return jax.shard_map(
        per_device, mesh=mesh, in_specs=in_specs, out_specs=out_specs, check_vma=False
    )
```

profile of v0, /device:TPU:0, one launch (start us, length us, event | category | flops | bytes accessed | tf_op | source)
XLA Modules:
  0.0 134.9 jit_solution(11475658209776853552)
XLA Ops:
  0.6 10.6 %all-gather.3 = bf16[8,4,16]{2,1,0:T(4,128)(2,1)S(1)} all-gather(bf16[1,4,16]{2,1,0:T(4,128)(2,1)} %bitcast.83), channel_id=3, replica_groups=mesh['ctx'=8,'qry'=4] {'ctx'}, dimensions={0}, use_global_device_ids=true | all-gather | bytes 1152 | tf_op jit(solution)/shard_map/all_gather | solution.py:39
  11.2 0.6 copy.20
  11.8 4.9 %all-to-all-start.1 = ((bf16[8,4,1,16]{3,0,2,1:T(8,128)(2,1)}), bf16[8,4,1,16]{3,0,2,1:T(8,128)(2,1)S(1)}, u32[]{:S(2)}, u32[]{:S(2)}) async-start(bf16[8,4,1,16]{3,0,2,1:T(8,128)(2,1)} %copy.20), calls=%async_computation.1 | async-start | bytes 16384 | tf_op jit(solution)/shard_map/all_to_all | solution.py:49
  16.7 8.6 %all-gather.4 = s32[8,1,32]{2,1,0:T(1,128)S(1)} all-gather(s32[1,1,32]{2,1,0:T(1,128)} %bitcast.84), channel_id=1, replica_groups=mesh['ctx'=8,'qry'=4] {'ctx'}, dimensions={0}, use_global_device_ids=true | all-gather | bytes 1152 | tf_op jit(solution)/shard_map/all_gather | solution.py:80
  25.3 0.3 convert_reduce_fusion
  25.6 0.2 select_reduce_fusion
  25.8 8.4 %all-gather.2 = bf16[8,4,2048]{2,1,0:T(4,128)(2,1)S(1)} all-gather(bf16[1,4,2048]{2,1,0:T(4,128)(2,1)} %bitcast.82), channel_id=2, replica_groups=mesh['ctx'=8,'qry'=4] {'ctx'}, dimensions={0}, use_global_device_ids=true | all-gather | bytes 147456 | tf_op jit(solution)/shard_map/all_gather | solution.py:38
  34.3 0.7 copy.18
  35.0 0.0 all-to-all-done.1
  35.0 5.1 %all-to-all-start = ((bf16[8,4,1,2048]{3,0,2,1:T(8,128)(2,1)}), bf16[8,4,1,2048]{3,0,2,1:T(8,128)(2,1)S(1)}, u32[]{:S(2)}, u32[]{:S(2)}) async-start(bf16[8,4,1,2048]{3,0,2,1:T(8,128)(2,1)} %copy.18), calls=%async_computation | async-start | bytes 262144 | tf_op jit(solution)/shard_map/all_to_all | solution.py:42
  40.1 0.1 reshape.281
  40.2 0.1 reshape.278
  40.2 6.3 %all-to-all-done = bf16[8,4,1,2048]{3,0,2,1:T(8,128)(2,1)S(1)} async-done(((bf16[8,4,1,2048]{3,0,2,1:T(8,128)(2,1)}), bf16[8,4,1,2048]{3,0,2,1:T(8,128)(2,1)S(1)}, u32[]{:S(2)}, u32[]{:S(2)}) %all-to-all-start) | async-done | bytes 131104 | tf_op jit(solution)/shard_map/all_to_all | solution.py:42
  46.5 0.1 copy.19
  46.6 0.1 reshape.266
  46.7 5.1 %while.13 = (s32[]{:T(128)}, bf16[8,2048]{1,0:T(8,128)(2,1)S(1)}, bf16[2048,128]{1,0:T(8,128)(2,1)}, bf16[512,128]{1,0:T(8,128)(2,1)S(1)}, f32[8,64]{1,0:T(8,128...) while((s32[]{:T(128)}, bf16[8,2048]{1,0:T(8,128)(2,1)S(1)}, bf16[2048,128]{1,0:T(8,128)(2,1)}, ...), condition=%wide.region_2.0_spmd, body=%wide.region_0.0_spmd.sunk | while | flops 67891208 | bytes 288915 | solution.py:70
  46.7 1.2 multiply_reduce_fusion.2
  48.0 1.2 multiply_reduce_fusion.2
  49.3 1.2 multiply_reduce_fusion.2
  50.5 1.2 multiply_reduce_fusion.2
  51.8 0.5 broadcast.203
  52.3 0.7 reduce.11
  53.0 0.6 reshape.309
  53.6 3.3 %all-to-all-start.2 = ((bf16[8,2,1024]{2,1,0:T(2,128)(2,1)}), bf16[8,2,1024]{2,1,0:T(2,128)(2,1)S(1)}, u32[]{:S(2)}, u32[]{:S(2)}) async-start(bf16[8,2,1024]{2,1,0:T(2,128)(2,1)} %reshape.309), calls=%async_computation.2 | async-start | bytes 65536 | tf_op jit(solution)/shard_map/all_to_all | solution.py:74
  57.0 3.1 %copy.23 = bf16[2048,576]{1,0:T(8,128)(2,1)S(1)} copy(bf16[2048,576]{0,1:T(8,128)(2,1)} %param.12) | data formatting | bytes 4718592 | tf_op args[4]
  60.1 3.5 %gather_fusion = bf16[64,64,576]{2,1,0:T(8,128)(2,1)} fusion(bf16[32,64,576]{2,1,0:T(8,128)(2,1)S(1)} %bitcast.71, s32[1024]{0:T(1024)S(1)} %pad_clamp_fusion.1), kind=kCustom, calls=%fused_computation | custom fusion | bytes 9437440 | tf_op jit(solution)/shard_map/gather | solution.py:88
  63.6 0.0 all-to-all-done.2
  63.6 0.0 copy-start
  63.6 0.0 copy-start.1
  63.6 4.8 %all-to-all-start.3 = ((bf16[8,8,64,576]{3,2,1,0:T(8,128)(2,1)}), bf16[8,8,64,576]{3,2,1,0:T(8,128)(2,1)}, u32[]{:S(2)}, u32[]{:S(2)}) async-start(bf16[8,8,64,576]{3,2,1,0:T(8,128)(2,1)} %bitcast.72), calls=%async_computation.3 | async-start | bytes 10485760 | tf_op jit(solution)/shard_map/all_to_all | solution.py:90
  68.4 0.0 copy-done
  68.4 0.9 reduce.10
  69.3 0.2 reshape.274
  69.4 0.0 copy-done.1
  69.5 0.2 convert_reduce_fusion.1
  69.7 0.7 reduce_max.23
  71.1 0.7 exponential_reduce_fusion
  73.2 0.7 subtract_add_fusion
  73.9 54.8 %all-to-all-done.3 = bf16[8,8,64,576]{3,2,1,0:T(8,128)(2,1)} async-done(((bf16[8,8,64,576]{3,2,1,0:T(8,128)(2,1)}), bf16[8,8,64,576]{3,2,1,0:T(8,128)(2,1)}, u32[]{:S(2)}, u32[]{:S(2)}) %all-to-all-start.3) | async-done | bytes 4718624 | tf_op jit(solution)/shard_map/all_to_all | solution.py:90
  128.7 3.5 %gather_fusion.1 = bf16[32,64,576]{2,1,0:T(8,128)(2,1)S(1)} fusion(bf16[64,64,576]{2,1,0:T(8,128)(2,1)} %bitcast.13, s32[1024]{0:T(1024)S(1)} %pad_clamp_fusion), kind=kCustom, calls=%fused_computation.1 | custom fusion | bytes 4718720 | tf_op jit(solution)/shard_map/gather | solution.py:93
  132.2 0.9 fusion.13
  133.1 0.3 fusion.5
  133.4 0.6 fusion.4
  134.0 0.9 copy.24
  (16 shorter events, 0.2 us)
Async XLA Ops:
  11.8 23.2 %all-to-all-start.1 = ((bf16[8,4,1,16]{3,0,2,1:T(8,128)(2,1)}), bf16[8,4,1,16]{3,0,2,1:T(8,128)(2,1)S(1)}, u32[]{:S(2)}, u32[]{:S(2)}) async-start(bf16[8,4,1,16]{3,0,2,1:T(8,128)(2,1)} %copy.20), calls=%async_computation.1 | async-start | bytes 16384 | tf_op jit(solution)/shard_map/all_to_all | solution.py:49
  35.0 11.5 %all-to-all-start = ((bf16[8,4,1,2048]{3,0,2,1:T(8,128)(2,1)}), bf16[8,4,1,2048]{3,0,2,1:T(8,128)(2,1)S(1)}, u32[]{:S(2)}, u32[]{:S(2)}) async-start(bf16[8,4,1,2048]{3,0,2,1:T(8,128)(2,1)} %copy.18), calls=%async_computation | async-start | bytes 262144 | tf_op jit(solution)/shard_map/all_to_all | solution.py:42
  53.6 10.0 %all-to-all-start.2 = ((bf16[8,2,1024]{2,1,0:T(2,128)(2,1)}), bf16[8,2,1024]{2,1,0:T(2,128)(2,1)S(1)}, u32[]{:S(2)}, u32[]{:S(2)}) async-start(bf16[8,2,1024]{2,1,0:T(2,128)(2,1)} %reshape.309), calls=%async_computation.2 | async-start | bytes 65536 | tf_op jit(solution)/shard_map/all_to_all | solution.py:74
  63.6 4.8 %copy-start = (bf16[1,73728]{1,0:T(2,128)(2,1)S(1)}, bf16[1,73728]{1,0:T(2,128)(2,1)}, u32[]{:S(2)}) copy-start(bf16[1,73728]{1,0:T(2,128)(2,1)} %param.11) | copy-start | bytes 442372
  63.6 5.8 %copy-start.1 = (s32[1,32]{1,0:T(1,128)S(1)}, s32[1,32]{1,0:T(1,128)}, u32[]{:S(2)}) copy-start(s32[1,32]{1,0:T(1,128)} %param.13) | copy-start | bytes 388
  63.6 65.1 %all-to-all-start.3 = ((bf16[8,8,64,576]{3,2,1,0:T(8,128)(2,1)}), bf16[8,8,64,576]{3,2,1,0:T(8,128)(2,1)}, u32[]{:S(2)}, u32[]{:S(2)}) async-start(bf16[8,8,64,576]{3,2,1,0:T(8,128)(2,1)} %bitcast.72), calls=%async_computation.3 | async-start | bytes 10485760 | tf_op jit(solution)/shard_map/all_to_all | solution.py:90
where the time goes:
time: 136 us; the launch traced here: 135 us
  waiting for transfers between devices  61.1 us (45%)
  blocking collectives  27.6 us (20%)
  starting transfers between devices  18.1 us (13%)
  local copies, waits for them, and re-layouts  14.1 us (10%)
  matrix products  6.35 us (5%)
  other arithmetic  4.78 us (4%)
  between operations  2.79 us (2%)
    all_to_all x1, waiting for transfers between devices, per_device(): lax.all_to_all(slot_keys, 'ctx', split_axis=0, concat_axis=0, tiled=True)  54.8 us
    all_gather x1, blocking collectives, per_device(): lax.all_gather(local_weight, 'ctx', axis=0, tiled=True)  10.6 us
    all_gather x1, blocking collectives, per_device(): group_ids = lax.all_gather(page_ids, 'ctx', axis=0, tiled=True)  8.63 us
    all_gather x1, blocking collectives, per_device(): lax.all_gather(local_query, 'ctx', axis=0, tiled=True)  8.42 us
    all_to_all x1, waiting for transfers between devices, per_device(): lax.all_to_all(every_query.reshape(shard_count, group_count, rows_dev, id...  6.25 us
    all_to_all x1, starting transfers between devices, per_device(): lax.all_to_all(every_query.reshape(shard_count, group_count, rows_dev, id...  5.07 us
    dot_general x4, matrix products, score_block(): lax.dot_general(flat_query, key_block, (((1,), (1,)), ((), ())), preferre...  4.91 us
    all_to_all x1, starting transfers between devices, per_device(): lax.all_to_all(every_weight.reshape(shard_count, group_count, rows_dev, i...  4.87 us
  transfers between devices with their start and end apart: 4, of which 2 were waited for; matrix products, arithmetic and copies ran while one was open for 9% of the time, Pallas kernels for 0%

commit v1 on v0

v1 whole, which is shorter than its diff:
```python
import functools

import jax
import jax.numpy as jnp
from jax import lax
from jax.experimental import pallas as pl
from jax.experimental.pallas import tpu as pltpu
from jax.sharding import PartitionSpec as P

H_IDX = 64
D_IDX = 128
H = 128
D_LAT = 512
D_ROPE = 64
QK_NOPE = 128
PAGE = 64

MESH = pl.DeviceIdType.MESH
LOG2E = 1.4426950408889634
NEG = -1e30


def flip(a, r, n):
    out, bit = 0, 1
    while bit < n:
        x, y = (a // bit) % 2, (r // bit) % 2
        out = out + bit * (x + y - 2 * x * y)
        bit *= 2
    return out


def repeat(lo, hi, body):
    if hi - lo <= 8:
        for i in range(lo, hi):
            body(i)
    else:

        def step(i, carry):
            body(i)
            return carry

        lax.fori_loop(lo, hi, step, 0)


def kernel(
    n, g, group, chunk, ichunk,
    mine_ref, cache_ref, keys_ref, query_ref,
    logp_ref, out_ref,
    zed, idx, kt, qr, logits, acc, osend, orecv, tsend, trecv, ssend, srecv,
    z_s, z_r, i_s, i_r, k_s, k_r, q_s, q_r, o_s, o_r, t_s, t_r, s_s, s_r, loc,
):
    c = lax.axis_index("ctx")
    z = lax.axis_index("qry")
    core = c % 2
    ctx_dev = keys_ref.shape[0]
    width = cache_ref.shape[0]
    half = H // 2
    hb = mine_ref.shape[2]

    barrier = pltpu.get_barrier_semaphore()

    def greet_z(r):
        pl.semaphore_signal(
            barrier, inc=1, device_id=(c, flip(z, r, g)), device_id_type=MESH
        )

    def greet_c(r):
        pl.semaphore_signal(
            barrier, inc=1, device_id=(flip(c, r, n), z), device_id_type=MESH
        )

    repeat(1, g, greet_z)
    repeat(1, n, greet_c)

    own_z = pltpu.make_async_copy(mine_ref.at[z], zed.at[z], loc.at[0])
    own_k = pltpu.make_async_copy(
        cache_ref, kt.at[core, pl.ds(0, width), :], loc.at[1]
    )
    own_q = pltpu.make_async_copy(query_ref.at[c // 2, core], qr.at[0], loc.at[2])
    own_z.start()
    own_k.start()
    own_q.start()

    def z_copy(r):
        peer = flip(z, r, g)
        return pltpu.make_async_remote_copy(
            src_ref=mine_ref.at[peer], dst_ref=zed.at[z],
            send_sem=z_s.at[r], recv_sem=z_r.at[r],
            device_id=(c, peer), device_id_type=MESH,
        )

    def k_copy():
        return pltpu.make_async_remote_copy(
            src_ref=cache_ref, dst_ref=kt.at[core, pl.ds(0, width), :],
            send_sem=k_s, recv_sem=k_r,
            device_id=(flip(c, 1, n), z), device_id_type=MESH,
        )

    def c_copy(src, dst, send, recv, r):
        return pltpu.make_async_remote_copy(
            src_ref=src, dst_ref=dst, send_sem=send.at[r], recv_sem=recv.at[r],
            device_id=(flip(c, r, n), z), device_id_type=MESH,
        )

    def q_copy(r):
        peer = flip(c, r, n)
        return c_copy(query_ref.at[peer // 2, peer % 2], qr.at[r], q_s, q_r, r)

    def i_copy(r):
        return c_copy(zed, idx.at[r], i_s, i_r, r)

    def o_copy(r):
        return c_copy(osend.at[r], orecv.at[r], o_s, o_r, r)

    def t_copy(r):
        return c_copy(tsend.at[r], trecv.at[r], t_s, t_r, r)

    def s_copy(r):
        return c_copy(ssend.at[r], srecv.at[c], s_s, s_r, r)

    pages_dev = ctx_dev // PAGE
    page_row = lax.broadcasted_iota(jnp.int32, (2 * pages_dev, ctx_dev), 0)
    page_col = lax.broadcasted_iota(jnp.int32, (2 * pages_dev, ctx_dev), 1) // PAGE
    for h in range(2):
        kt[h, width:, :] = jnp.where(page_row == page_col + h * pages_dev, 1.0, 0.0).astype(
            jnp.bfloat16
        )

    pl.semaphore_wait(barrier, (g - 1) + (n - 1))

    repeat(1, g, lambda r: z_copy(r).start())
    k_copy().start()
    first = max(2, n * 3 // 4)
    repeat(1, first, lambda r: q_copy(r).start())
    own_z.wait()
    repeat(1, g, lambda r: z_copy(r).wait_recv())
    own_i = pltpu.make_async_copy(zed, idx.at[0], loc.at[3])
    own_i.start()
    repeat(1, n, lambda r: i_copy(r).start())
    repeat(first, n, lambda r: q_copy(r).start())

    own_i.wait()
    repeat(1, n, lambda r: i_copy(r).wait_recv())

    def index_rows(r):
        rows = idx[r]
        q_rows = rows[:, 0].reshape(g * hb, D_IDX)
        w_rows = rows[:, 1].reshape(g * hb, D_IDX).astype(jnp.float32)
        w_wide = jnp.concatenate([w_rows] * (ichunk // D_IDX), axis=1)

        def block(s, carry):
            at = pl.ds(pl.multiple_of(s * ichunk, ichunk), ichunk)
            dots = lax.dot_general(
                q_rows, keys_ref[at, :], (((1,), (1,)), ((), ())),
                preferred_element_type=jnp.float32,
            )
            ssend[r, :, at] = jnp.sum(jnp.maximum(dots, 0.0) * w_wide, axis=0, keepdims=True)
            return carry

        lax.fori_loop(0, ctx_dev // ichunk, block, 0)

    repeat(0, n, index_rows)
    repeat(1, n, lambda r: s_copy(r).start())
    own_s = pltpu.make_async_copy(ssend.at[0], srecv.at[c], loc.at[4])
    own_s.start()

    own_k.wait()
    own_q.wait()
    k_copy().wait_recv()
    per = ctx_dev // chunk
    scale = ((QK_NOPE + D_ROPE) ** -0.5) * LOG2E
    m_rows = group * half

    def rows_of(b):
        for j in range(group):
            r = b * group + j
            if isinstance(r, int):
                if r > 0:
                    q_copy(r).wait_recv()
            else:

                @pl.when(r > 0)
                def _():
                    q_copy(r).wait_recv()

        def part_one(s, peak):
            keys = pl.ds(pl.multiple_of((s % per) * chunk, chunk), chunk)
            dots = jnp.dot(
                qr[pl.ds(b * group, group)].reshape(m_rows, qr.shape[2]),
                kt[s // per, :, keys],
                preferred_element_type=jnp.float32,
            ) * scale
            logits[s] = dots
            for t in range(chunk // 128):
                peak = jnp.maximum(peak, dots[:, t * 128 : (t + 1) * 128])
            return peak

        peak = lax.fori_loop(
            0, 2 * per, part_one, jnp.full((m_rows, 128), -jnp.inf, jnp.float32)
        )
        top = jnp.max(peak, axis=1, keepdims=True)
        acc[...] = jnp.zeros_like(acc)

        def part_two(s, total):
            keys = pl.ds(pl.multiple_of((s % per) * chunk, chunk), chunk)
            expo = jnp.exp2(logits[s] - top)
            for t in range(chunk // 128):
                total = total + expo[:, t * 128 : (t + 1) * 128]
            acc[...] += lax.dot_general(
                expo.astype(jnp.bfloat16), kt[s // per, :D_LAT, keys],
                (((1,), (1,)), ((), ())), preferred_element_type=jnp.float32,
            )
            return total

        total = lax.fori_loop(0, 2 * per, part_two, jnp.zeros((m_rows, 128), jnp.float32))
        mass = jnp.sum(total, axis=1, keepdims=True)
        lane = lax.broadcasted_iota(jnp.int32, (m_rows, 128), 1)
        stats = jnp.where(lane == 0, top, mass)
        osend[pl.ds(b * group, group)] = acc[...].astype(jnp.bfloat16).reshape(
            group, half, D_LAT
        )
        for j in range(group):
            turned = jnp.transpose(stats[j * half : (j + 1) * half, :])
            tsend[b * group + j] = jnp.concatenate([turned[:8], turned[:8]], axis=1)
        for j in range(group):
            r = b * group + j
            if isinstance(r, int):
                if r > 0:
                    t_copy(r).start()
                    o_copy(r).start()
            else:

                @pl.when(r > 0)
                def _():
                    t_copy(r).start()
                    o_copy(r).start()

    repeat(0, n // group, rows_of)

    own_s.wait()

    def take_scores(r):
        peer = flip(c, r, n)
        c_copy(ssend.at[r], srecv.at[peer], s_s, s_r, r).wait_recv()

    repeat(1, n, take_scores)
    table = srecv[...]
    row_max = jnp.max(table)
    row_total = jnp.sum(jnp.exp(table - row_max), keepdims=True)
    logp_ref[...] = table - (row_max + jnp.log(row_total)) + jnp.log(
        jnp.full((1, 1, 1), n * ctx_dev, jnp.float32)
    )

    def arrive(r):
        t_copy(r).wait_recv()
        o_copy(r).wait_recv()

    repeat(1, n, arrive)
    for parity in range(2):
        tops, masses = [], []
        for r in range(parity, n, 2):
            stat = tsend[r] if r == 0 else trecv[r]
            col = jnp.transpose(stat)[:half]
            tops.append(col[:, 0:1])
            masses.append(col[:, 1:2])
        best = functools.reduce(jnp.maximum, tops)
        weights = [jnp.exp2(t - best) for t in tops]
        mass = functools.reduce(jnp.add, [w * l for w, l in zip(weights, masses)])
        mixed = jnp.zeros((half, D_LAT), jnp.float32)
        for s, r in enumerate(range(parity, n, 2)):
            value = osend[r] if r == 0 else orecv[r]
            mixed = mixed + value.astype(jnp.float32) * (weights[s] / mass)
        out_ref[(core + parity) % 2] = mixed.astype(jnp.bfloat16)

    repeat(1, g, lambda r: z_copy(r).wait_send())
    k_copy().wait_send()

    def sent(r):
        q_copy(r).wait_send()
        i_copy(r).wait_send()
        o_copy(r).wait_send()
        t_copy(r).wait_send()
        s_copy(r).wait_send()

    repeat(1, n, sent)


def per_device(n, g, idx_query, idx_weight, idx_keys, q_latent, latent_cache, page_ids):
    hb = H_IDX // g
    ctx_dev, width = idx_keys.shape[0], latent_cache.shape[1]
    pages_dev = ctx_dev // PAGE
    chips = n // 2
    group, chunk, ichunk = 4, 512, 512

    heads = idx_query.reshape(g, 1, hb, D_IDX)
    gains = jnp.broadcast_to(idx_weight.reshape(g, 1, hb, 1), heads.shape)
    mine = jnp.concatenate([heads, gains], axis=1)
    chip_pages = jnp.arange(n * pages_dev, dtype=jnp.int32)
    hit = jnp.any(page_ids.reshape(-1, 1) == chip_pages[None, :], axis=0)
    flags = jnp.where(hit, 0.0, NEG).astype(jnp.bfloat16).reshape(chips, 1, 2 * pages_dev)
    query = jnp.concatenate(
        [
            jnp.broadcast_to(q_latent.reshape(1, H, width), (chips, H, width)),
            jnp.broadcast_to(flags, (chips, H, 2 * pages_dev)),
        ],
        axis=2,
    ).reshape(chips, 2, H // 2, width + 2 * pages_dev)

    full = width + 2 * pages_dev
    half = H // 2
    dma = pltpu.SemaphoreType.DMA
    vmem = pl.BlockSpec(memory_space=pltpu.VMEM)
    logp, out = pl.pallas_call(
        functools.partial(kernel, n, g, group, chunk, ichunk),
        out_shape=(
            jax.ShapeDtypeStruct((n, 1, ctx_dev), jnp.float32),
            jax.ShapeDtypeStruct((2, half, D_LAT), jnp.bfloat16),
        ),
        in_specs=[vmem, pl.BlockSpec(memory_space=pl.ANY), vmem, vmem],
        out_specs=(vmem, vmem),
        scratch_shapes=[
            pltpu.VMEM((g, 2, hb, D_IDX), jnp.bfloat16),
            pltpu.VMEM((n, g, 2, hb, D_IDX), jnp.bfloat16),
            pltpu.VMEM((2, full, ctx_dev), jnp.bfloat16),
            pltpu.VMEM((n, half, full), jnp.bfloat16),
            pltpu.VMEM((2 * ctx_dev // chunk, group * half, chunk), jnp.float32),
            pltpu.VMEM((group * half, D_LAT), jnp.float32),
            pltpu.VMEM((n, half, D_LAT), jnp.bfloat16),
            pltpu.VMEM((n, half, D_LAT), jnp.bfloat16),
            pltpu.VMEM((n, 8, 128), jnp.float32),
            pltpu.VMEM((n, 8, 128), jnp.float32),
            pltpu.VMEM((n, 1, ctx_dev), jnp.float32),
            pltpu.VMEM((n, 1, ctx_dev), jnp.float32),
            dma((g,)), dma((g,)),
            dma((n,)), dma((n,)),
            dma, dma,
            dma((n,)), dma((n,)),
            dma((n,)), dma((n,)),
            dma((n,)), dma((n,)),
            dma((n,)), dma((n,)),
            dma((5,)),
        ],
        compiler_params=pltpu.CompilerParams(
            collective_id=0, has_side_effects=True, vmem_limit_bytes=60 * 1024 * 1024
        ),
    )(mine, latent_cache.T, idx_keys, query)
    return logp.reshape(1, n * ctx_dev), out.reshape(1, H * D_LAT)


def solution(mesh):
    in_specs = (
        P("ctx", "qry"),
        P("ctx", "qry"),
        P("ctx", None),
        P(("ctx", "qry"), None),
        P("ctx", None),
        P(("ctx", "qry"), None),
    )
    out_specs = (P(("ctx", "qry"), None), P(("ctx", "qry"), None))
    return jax.shard_map(
        functools.partial(per_device, mesh.shape["ctx"], mesh.shape["qry"]),
        mesh=mesh, in_specs=in_specs, out_specs=out_specs, check_vma=False,
    )
```

time: 136 us -> 52.2 us (0.38)
  waiting for transfers between devices: 61.1 us -> 0 us
  Pallas kernels: 0 us -> 44.3 us
  blocking collectives: 27.6 us -> 0 us
  starting transfers between devices: 18.1 us -> 0 us
  local copies, waits for them, and re-layouts: 14.1 us -> 3.55 us
  matrix products: 6.35 us -> 0 us
  between operations: 2.79 us -> 0.7 us
    all_to_all x4 -> x0, waiting for transfers between devices: 61.1 us -> none  [the longest x1 54.8 us: per_device(): lax.all_to_all(slot_keys, 'ctx', split_axis=0, concat_axis=0, tiled=True)]
    pallas_call x0 -> x1, Pallas kernels: none -> 44.3 us  [per_device(): pl.pallas_call(functools.partial(kernel, n, g, group, chunk, ichunk), out...]
    all_gather x3 -> x0, blocking collectives: 27.6 us -> none  [the longest x1 10.6 us: per_device(): lax.all_gather(local_weight, 'ctx', axis=0, tiled=True)]
    all_to_all x4 -> x0, starting transfers between devices: 18.1 us -> none  [the longest x1 5.07 us: per_device(): lax.all_to_all(every_query.reshape(shard_count, group_count, rows_dev, id...]
    gather x2 -> x0, local copies, waits for them, and re-layouts: 7.03 us -> none  [the longest x1 3.53 us: per_device(): slot_keys = page_store[slot_page]]
    dot_general x6 -> x0, matrix products: 6.35 us -> none  [the longest x4 4.91 us: score_block(): lax.dot_general(flat_query, key_block, (((1,), (1,)), ((), ())), preferre...]
    unnamed x8, local copies, waits for them, and re-layouts: 4.66 us -> 1.49 us
    reduce_sum x5 -> x0, other arithmetic: 1.73 us -> none  [the longest x1 0.74 us: per_device(): row_total = jnp.sum(jnp.exp(score_table - row_max), axis=1, keepdims=True)]
  transfers between devices with their start and end apart: 4 -> 0, of which waited for: 2 -> 0; matrix products, arithmetic and copies ran while one was open for 9% -> 0% of each run, Pallas kernels for 0% -> 0%
where the time goes in v1:
time: 52.2 us; the launch traced here: 52 us
  Pallas kernels  44.3 us (85%)
  local copies, waits for them, and re-layouts  3.55 us (7%)
  other arithmetic  3.45 us (7%)
  between operations  0.7 us (1%)
    pallas_call x1, Pallas kernels, per_device(): pl.pallas_call(functools.partial(kernel, n, g, group, chunk, ichunk), out...  44.3 us
    unnamed x1, other arithmetic  1.78 us
    reshape x1, local copies, waits for them, and re-layouts, per_device(): return (logp.reshape(1, n * ctx_dev), out.reshape(1, H * D_LAT))  1.67 us
    unnamed x8, local copies, waits for them, and re-layouts  1.49 us

profile of v1, /device:TPU:0, one launch (start us, length us, event | category | flops | bytes accessed | tf_op | source)
XLA Modules:
  0.0 52.0 jit_solution(11347705187666386372)
XLA Ops:
  0.6 0.0 copy-start.2
  0.6 1.8 %reduce = bf16[73728]{0:T(1024)(128)(2,1)S(1)} reduce(bf16[1,73728]{1,0:T(2,128)(2,1)} %param.9, bf16[]{:T(256)} %constant.10), dimensions={0}, to_apply=%param.9.reduce_sub_computation | reduce | bytes 294914 | tf_op args[3]
  2.4 0.0 copy-start
  2.4 0.0 copy-start.1
  2.4 0.2 broadcast_in_dim.27
  2.6 0.1 broadcast_in_dim.28
  2.7 0.0 copy-done.2
  2.7 0.1 fusion
  2.8 0.1 convert_element_type.11
  2.9 0.9 %pad_maximum_fusion = bf16[4,128,640]{2,1,0:T(8,128)(2,1)} fusion(bf16[4,128,64]{2,1,0:T(8,128)(2,1)S(1)} %broadcast_in_dim.31, bf16[4,128,576]{2,1,0:T(8,128)(2,1)S(1)} %broadcast_in_dim.28), kind=kLoop, calls=%fused_computation | loop fusion | flops 1310720 | bytes 1310720 | tf_op jit(solution)/shard_map/concatenate | solution.py:301
  3.8 0.0 copy-done
  3.8 0.0 copy-done.1
  3.8 0.1 broadcast_in_dim.26
  3.9 0.6 %pad_maximum_fusion.1.mine_ref = bf16[4,2,16,128]{3,2,1,0:T(8,128)(2,1)} fusion(bf16[4,1,16,128]{3,2,1,0:T(8,128)(2,1)S(1)} %broadcast_in_dim.26, bf16[4,1,16,128]{3,2,1,0:T(8,128)(2,1)S(1)} %bitcast.12), kind=kLoop, calls=%fused_computation.1 | loop fusion | flops 16384 | bytes 65536 | tf_op jit(solution)/shard_map/concatenate | solution.py:297
  4.5 44.3 %shard_map.77 = (f32[8,1,2048]{2,1,0:T(1,128)}, bf16[2,64,512]{2,1,0:T(8,128)(2,1)}) custom-call(bf16[4,2,16,128]{3,2,1,0:T(8,128)(2,1)} %pad_maximum_fusion.1.mine_ref, bf16[576,2048]{1,0:T(8,128)(2,1)} %bitcast.10, bf16[2048,128]{1,0:T(8,128)(2,1)} %keys_ref.1, bf16[4,2,64,640]{3,2,1,0:T(8,128)(2,1)} %bitcast.9), custom_call_target="tpu_custom_call" | custom-call | tf_op jit(solution)/shard_map/pallas_call | solution.py:313
  48.9 1.7 %reshape.38 = bf16[1,65536]{1,0:T(2,128)(2,1)} reshape(bf16[2,64,512]{2,1,0:T(8,128)(2,1)} %get-tuple-element.5) | data formatting | bytes 262144 | tf_op jit(solution)/shard_map/reshape | solution.py:347
  50.5 1.5 %copy.12 = f32[1,16384]{1,0:T(1,128)} copy(f32[1,16384]{1,0:T(1,128)} %bitcast.11) | data formatting | bytes 131072
  (3 shorter events, 0.0 us)
Async XLA Ops:
  0.6 2.0 %copy-start.2 = (s32[1,32]{1,0:T(1,128)S(1)}, s32[1,32]{1,0:T(1,128)}, u32[]{:S(2)}) copy-start(s32[1,32]{1,0:T(1,128)} %param.11) | copy-start | bytes 388
  2.4 1.4 %copy-start = (bf16[4,2048]{1,0:T(4,128)(2,1)S(1)}, bf16[4,2048]{1,0:T(4,128)(2,1)}, u32[]{:S(2)}) copy-start(bf16[4,2048]{1,0:T(4,128)(2,1)} %param.6) | copy-start | bytes 49156
  2.4 1.4 %copy-start.1 = (bf16[4,16]{1,0:T(4,128)(2,1)S(1)}, bf16[4,16]{1,0:T(4,128)(2,1)}, u32[]{:S(2)}) copy-start(bf16[4,16]{1,0:T(4,128)(2,1)} %param.7) | copy-start | bytes 388

commit v2 on v1

--- a/solution.py
+++ b/solution.py
@@ -43,9 +43,10 @@
 
 
 def kernel(
-    n, g, group, chunk, ichunk,
-    mine_ref, cache_ref, keys_ref, query_ref,
+    n, g, group, chunk, ichunk, unroll,
+    heads_ref, gains_ref, cache_ref, keys_ref, latent_ref, pages_ref,
     logp_ref, out_ref,
+    head_rows, mine_ref, pairs, query_ref, flat_query, wide_gains,
     zed, idx, kt, qr, logits, acc, osend, orecv, tsend, trecv, ssend, srecv,
     z_s, z_r, i_s, i_r, k_s, k_r, q_s, q_r, o_s, o_r, t_s, t_r, s_s, s_r, loc,
 ):
@@ -72,14 +73,50 @@
     repeat(1, g, greet_z)
     repeat(1, n, greet_c)
 
-    own_z = pltpu.make_async_copy(mine_ref.at[z], zed.at[z], loc.at[0])
     own_k = pltpu.make_async_copy(
         cache_ref, kt.at[core, pl.ds(0, width), :], loc.at[1]
     )
-    own_q = pltpu.make_async_copy(query_ref.at[c // 2, core], qr.at[0], loc.at[2])
-    own_z.start()
     own_k.start()
-    own_q.start()
+
+    for h in range(hb):
+        piece = heads_ref[:, h * D_IDX : (h + 1) * D_IDX].astype(jnp.float32)
+        for r in range(g):
+            head_rows[r, h : h + 1, :] = piece[r : r + 1]
+    eye = lax.broadcasted_iota(jnp.int32, (hb, hb), 0) == lax.broadcasted_iota(
+        jnp.int32, (hb, hb), 1
+    )
+    gains = gains_ref[...].astype(jnp.float32)
+    for r in range(g):
+        mine_ref[r, 0] = head_rows[r].astype(jnp.bfloat16)
+        gain = jnp.sum(jnp.where(eye, gains[r : r + 1], 0.0), axis=1, keepdims=True)
+        mine_ref[r, 1] = jnp.broadcast_to(gain, (hb, D_IDX)).astype(jnp.bfloat16)
+
+    full = query_ref.shape[3]
+    for p in range(half):
+        pairs[p : p + 1, :] = latent_ref[:, p * 2 * width : (p + 1) * 2 * width].astype(
+            jnp.float32
+        )
+    topp = pages_ref.shape[1]
+    eye = lax.broadcasted_iota(jnp.int32, (topp, topp), 0) == lax.broadcasted_iota(
+        jnp.int32, (topp, topp), 1
+    )
+    ids = jnp.sum(
+        jnp.where(eye, pages_ref[...].astype(jnp.float32), 0.0), axis=1, keepdims=True
+    )
+    spare = 2 * (ctx_dev // PAGE)
+    lane = lax.broadcasted_iota(jnp.int32, (topp, 128), 1)
+    tail_lane = lax.broadcasted_iota(jnp.int32, (half, 128), 1)
+    even = pairs[:, :full]
+    odd = pltpu.roll(pairs[:, 2 * width - full :], width, 1)
+    for j in range(n // 2):
+        page = (lane - (128 - spare) + j * spare).astype(jnp.float32)
+        hit = jnp.max(jnp.where(ids == page, 1.0, 0.0), axis=0, keepdims=True)
+        flags = jnp.where(hit > 0.5, 0.0, NEG)
+        for h, rows in enumerate((even, odd)):
+            query_ref[j, h, :, : full - 128] = rows[:, : full - 128].astype(jnp.bfloat16)
+            query_ref[j, h, :, full - 128 :] = jnp.where(
+                tail_lane < 128 - spare, rows[:, full - 128 :], flags
+            ).astype(jnp.bfloat16)
 
     def z_copy(r):
         peer = flip(z, r, g)
@@ -128,6 +165,10 @@
 
     pl.semaphore_wait(barrier, (g - 1) + (n - 1))
 
+    own_z = pltpu.make_async_copy(mine_ref.at[z], zed.at[z], loc.at[0])
+    own_q = pltpu.make_async_copy(query_ref.at[c // 2, core], qr.at[0], loc.at[2])
+    own_z.start()
+    own_q.start()
     repeat(1, g, lambda r: z_copy(r).start())
     k_copy().start()
     first = max(2, n * 3 // 4)
@@ -139,30 +180,45 @@
     repeat(1, n, lambda r: i_copy(r).start())
     repeat(first, n, lambda r: q_copy(r).start())
 
-    own_i.wait()
-    repeat(1, n, lambda r: i_copy(r).wait_recv())
-
-    def index_rows(r):
-        rows = idx[r]
-        q_rows = rows[:, 0].reshape(g * hb, D_IDX)
-        w_rows = rows[:, 1].reshape(g * hb, D_IDX).astype(jnp.float32)
-        w_wide = jnp.concatenate([w_rows] * (ichunk // D_IDX), axis=1)
+    def index_rows():
+        own_i.wait()
+        repeat(1, n, lambda r: i_copy(r).wait_recv())
+        count = g * hb
+
+        def lay(r):
+            rows = idx[r]
+            flat_query[r] = rows[:, 0].reshape(count, D_IDX)
+            wide_gains[r] = rows[:, 1].reshape(count, D_IDX).astype(jnp.float32)
+
+        repeat(0, n, lay)
 
         def block(s, carry):
             at = pl.ds(pl.multiple_of(s * ichunk, ichunk), ichunk)
-            dots = lax.dot_general(
-                q_rows, keys_ref[at, :], (((1,), (1,)), ((), ())),
-                preferred_element_type=jnp.float32,
-            )
-            ssend[r, :, at] = jnp.sum(jnp.maximum(dots, 0.0) * w_wide, axis=0, keepdims=True)
+            keys = keys_ref[at, :]
+            for b in range(n // 4):
+                dots = lax.dot_general(
+                    flat_query[4 * b : 4 * b + 4].reshape(4 * count, D_IDX), keys,
+                    (((1,), (1,)), ((), ())), preferred_element_type=jnp.float32,
+                )
+                for j in range(4):
+                    r = 4 * b + j
+                    gain = wide_gains[r]
+                    sums = [
+                        jnp.sum(
+                            jnp.maximum(
+                                dots[j * count : (j + 1) * count, t * 128 : (t + 1) * 128], 0.0
+                            ) * gain,
+                            axis=0, keepdims=True,
+                        )
+                        for t in range(ichunk // 128)
+                    ]
+                    ssend[r, :, at] = jnp.concatenate(sums, axis=1)
             return carry
 
         lax.fori_loop(0, ctx_dev // ichunk, block, 0)
-
-    repeat(0, n, index_rows)
-    repeat(1, n, lambda r: s_copy(r).start())
+        repeat(1, n, lambda r: s_copy(r).start())
+
     own_s = pltpu.make_async_copy(ssend.at[0], srecv.at[c], loc.at[4])
-    own_s.start()
 
     own_k.wait()
     own_q.wait()
@@ -196,7 +252,7 @@
             return peak
 
         peak = lax.fori_loop(
-            0, 2 * per, part_one, jnp.full((m_rows, 128), -jnp.inf, jnp.float32)
+            0, 2 * per, part_one, jnp.full((m_rows, 128), -jnp.inf, jnp.float32), unroll=unroll
         )
         top = jnp.max(peak, axis=1, keepdims=True)
         acc[...] = jnp.zeros_like(acc)
@@ -212,7 +268,7 @@
             )
             return total
 
-        total = lax.fori_loop(0, 2 * per, part_two, jnp.zeros((m_rows, 128), jnp.float32))
+        total = lax.fori_loop(0, 2 * per, part_two, jnp.zeros((m_rows, 128), jnp.float32), unroll=unroll)
         mass = jnp.sum(total, axis=1, keepdims=True)
         lane = lax.broadcasted_iota(jnp.int32, (m_rows, 128), 1)
         stats = jnp.where(lane == 0, top, mass)
@@ -235,7 +291,10 @@
                     t_copy(r).start()
                     o_copy(r).start()
 
-    repeat(0, n // group, rows_of)
+    rows_of(0)
+    index_rows()
+    own_s.start()
+    repeat(1, n // group, rows_of)
 
     own_s.wait()
 
@@ -256,6 +315,7 @@
         o_copy(r).wait_recv()
 
     repeat(1, n, arrive)
+    mixes = []
     for parity in range(2):
         tops, masses = [], []
         for r in range(parity, n, 2):
@@ -270,7 +330,12 @@
         for s, r in enumerate(range(parity, n, 2)):
             value = osend[r] if r == 0 else orecv[r]
             mixed = mixed + value.astype(jnp.float32) * (weights[s] / mass)
-        out_ref[(core + parity) % 2] = mixed.astype(jnp.bfloat16)
+        mixes.append(mixed)
+
+    for h in range(2):
+        out_ref[:, h * D_LAT : (h + 1) * D_LAT] = jnp.where(
+            core == h, mixes[0], mixes[1]
+        ).astype(jnp.bfloat16)
 
     repeat(1, g, lambda r: z_copy(r).wait_send())
     k_copy().wait_send()
@@ -290,35 +355,26 @@
     ctx_dev, width = idx_keys.shape[0], latent_cache.shape[1]
     pages_dev = ctx_dev // PAGE
     chips = n // 2
-    group, chunk, ichunk = 4, 512, 512
-
-    heads = idx_query.reshape(g, 1, hb, D_IDX)
-    gains = jnp.broadcast_to(idx_weight.reshape(g, 1, hb, 1), heads.shape)
-    mine = jnp.concatenate([heads, gains], axis=1)
-    chip_pages = jnp.arange(n * pages_dev, dtype=jnp.int32)
-    hit = jnp.any(page_ids.reshape(-1, 1) == chip_pages[None, :], axis=0)
-    flags = jnp.where(hit, 0.0, NEG).astype(jnp.bfloat16).reshape(chips, 1, 2 * pages_dev)
-    query = jnp.concatenate(
-        [
-            jnp.broadcast_to(q_latent.reshape(1, H, width), (chips, H, width)),
-            jnp.broadcast_to(flags, (chips, H, 2 * pages_dev)),
-        ],
-        axis=2,
-    ).reshape(chips, 2, H // 2, width + 2 * pages_dev)
-
+    group, chunk, ichunk, unroll = 4, 1024, 256, True
     full = width + 2 * pages_dev
     half = H // 2
     dma = pltpu.SemaphoreType.DMA
     vmem = pl.BlockSpec(memory_space=pltpu.VMEM)
     logp, out = pl.pallas_call(
-        functools.partial(kernel, n, g, group, chunk, ichunk),
+        functools.partial(kernel, n, g, group, chunk, ichunk, unroll),
         out_shape=(
             jax.ShapeDtypeStruct((n, 1, ctx_dev), jnp.float32),
-            jax.ShapeDtypeStruct((2, half, D_LAT), jnp.bfloat16),
+            jax.ShapeDtypeStruct((half, 2 * D_LAT), jnp.bfloat16),
         ),
-        in_specs=[vmem, pl.BlockSpec(memory_space=pl.ANY), vmem, vmem],
+        in_specs=[vmem, vmem, pl.BlockSpec(memory_space=pl.ANY), vmem, vmem, vmem],
         out_specs=(vmem, vmem),
         scratch_shapes=[
+            pltpu.VMEM((g, hb, D_IDX), jnp.float32),
+            pltpu.VMEM((g, 2, hb, D_IDX), jnp.bfloat16),
+            pltpu.VMEM((half, 2 * width), jnp.float32),
+            pltpu.VMEM((chips, 2, half, full), jnp.bfloat16),
+            pltpu.VMEM((n, g * hb, D_IDX), jnp.bfloat16),
+            pltpu.VMEM((n, g * hb, D_IDX), jnp.float32),
             pltpu.VMEM((g, 2, hb, D_IDX), jnp.bfloat16),
             pltpu.VMEM((n, g, 2, hb, D_IDX), jnp.bfloat16),
             pltpu.VMEM((2, full, ctx_dev), jnp.bfloat16),
@@ -343,7 +399,7 @@
         compiler_params=pltpu.CompilerParams(
             collective_id=0, has_side_effects=True, vmem_limit_bytes=60 * 1024 * 1024
         ),
-    )(mine, latent_cache.T, idx_keys, query)
+    )(idx_query, idx_weight, latent_cache.T, idx_keys, q_latent, page_ids)
     return logp.reshape(1, n * ctx_dev), out.reshape(1, H * D_LAT)
 
 

time: 52.2 us -> 35.9 us (0.69)
  Pallas kernels: 44.3 us -> 31.8 us
  other arithmetic: 3.45 us -> 0 us
    pallas_call x1, Pallas kernels: 44.3 us -> 31.8 us  [per_device(): pl.pallas_call(functools.partial(kernel, n, g, group, chunk, ichunk, unro...]
    unnamed x8 -> x2, local copies, waits for them, and re-layouts: 1.49 us -> 3.28 us
    unnamed x1 -> x0, other arithmetic: 1.78 us -> none
    reshape x1 -> x0, local copies, waits for them, and re-layouts: 1.67 us -> none  [per_device(): return (logp.reshape(1, n * ctx_dev), out.reshape(1, H * D_LAT))]
    concatenate x2 -> x0, other arithmetic: 1.57 us -> none  [the longest x1 0.95 us: per_device(): jnp.concatenate([jnp.broadcast_to(q_latent.reshape(1, H, width), (chips,...]
where the time goes in v2:
time: 35.9 us; the launch traced here: 35.7 us
  Pallas kernels  31.8 us (89%)
  local copies, waits for them, and re-layouts  3.28 us (9%)
  between operations  0.64 us (2%)
    pallas_call x1, Pallas kernels, per_device(): pl.pallas_call(functools.partial(kernel, n, g, group, chunk, ichunk, unro...  31.8 us
    unnamed x2, local copies, waits for them, and re-layouts  3.28 us

profile of v2, /device:TPU:0, one launch (start us, length us, event | category | flops | bytes accessed | tf_op | source)
XLA Modules:
  0.0 35.7 jit_solution(9727565478779791314)
XLA Ops:
  0.6 31.8 %shard_map.77 = (f32[8,1,2048]{2,1,0:T(1,128)}, bf16[64,1024]{1,0:T(8,128)(2,1)}) custom-call(bf16[4,2048]{1,0:T(4,128)(2,1)} %heads_ref.1, bf16[4,16]{1,0:T(4,128)(2,1)} %gains_ref.1, bf16[576,2048]{1,0:T(8,128)(2,1)} %bitcast.5, bf16[2048,128]{1,0:T(8,128)(2,1)} %keys_ref.1, bf16[1,73728]{1,0:T(2,128)(2,1)} %latent_ref.1, s32[1,32]{1,0:T(1,128)} %pages_ref.1), custom_call_target="tpu_custom_call" | custom-call | tf_op jit(solution)/shard_map/pallas_call | solution.py:363
  32.4 1.8 %copy.8 = bf16[1,1,64,1024]{3,1,2,0:T(2,128)(2,1)} copy(bf16[1,1,64,1024]{3,2,1,0:T(8,128)(2,1)} %bitcast.7) | data formatting | bytes 262144
  34.2 1.5 %copy.10 = f32[1,16384]{1,0:T(1,128)} copy(f32[1,16384]{1,0:T(1,128)} %bitcast.8) | data formatting | bytes 131072

commit v3 on v2

--- a/solution.py
+++ b/solution.py
@@ -47,12 +47,13 @@
     heads_ref, gains_ref, cache_ref, keys_ref, latent_ref, pages_ref,
     logp_ref, out_ref,
     head_rows, mine_ref, pairs, query_ref, flat_query, wide_gains,
-    zed, idx, kt, qr, logits, acc, osend, orecv, tsend, trecv, ssend, srecv,
-    z_s, z_r, i_s, i_r, k_s, k_r, q_s, q_r, o_s, o_r, t_s, t_r, s_s, s_r, loc,
+    zed, idx, keys_all, kt, qr, logits, acc, osend, orecv, tsend, trecv, ssend, srecv,
+    z_s, z_r, i_s, i_r, k_s, k_r, q_s, q_r, o_s, o_r, t_s, t_r, s_s, s_r, e_s, e_r, loc,
 ):
     c = lax.axis_index("ctx")
     z = lax.axis_index("qry")
     core = c % 2
+    chips = n // 2
     ctx_dev = keys_ref.shape[0]
     width = cache_ref.shape[0]
     half = H // 2
@@ -77,6 +78,8 @@
         cache_ref, kt.at[core, pl.ds(0, width), :], loc.at[1]
     )
     own_k.start()
+    own_e = pltpu.make_async_copy(keys_ref, keys_all.at[core], loc.at[5])
+    own_e.start()
 
     for h in range(hb):
         piece = heads_ref[:, h * D_IDX : (h + 1) * D_IDX].astype(jnp.float32)
@@ -133,6 +136,13 @@
             device_id=(flip(c, 1, n), z), device_id_type=MESH,
         )
 
+    def e_copy():
+        return pltpu.make_async_remote_copy(
+            src_ref=keys_ref, dst_ref=keys_all.at[core],
+            send_sem=e_s, recv_sem=e_r,
+            device_id=(flip(c, 1, n), z), device_id_type=MESH,
+        )
+
     def c_copy(src, dst, send, recv, r):
         return pltpu.make_async_remote_copy(
             src_ref=src, dst_ref=dst, send_sem=send.at[r], recv_sem=recv.at[r],
@@ -143,8 +153,14 @@
         peer = flip(c, r, n)
         return c_copy(query_ref.at[peer // 2, peer % 2], qr.at[r], q_s, q_r, r)
 
-    def i_copy(r):
-        return c_copy(zed, idx.at[r], i_s, i_r, r)
+    def row_copy(src, dst, send, recv, m):
+        return pltpu.make_async_remote_copy(
+            src_ref=src, dst_ref=dst, send_sem=send.at[m], recv_sem=recv.at[m],
+            device_id=(2 * flip(c // 2, m, chips) + core, z), device_id_type=MESH,
+        )
+
+    def i_copy(m):
+        return row_copy(zed, idx.at[m], i_s, i_r, m)
 
     def o_copy(r):
         return c_copy(osend.at[r], orecv.at[r], o_s, o_r, r)
@@ -152,8 +168,8 @@
     def t_copy(r):
         return c_copy(tsend.at[r], trecv.at[r], t_s, t_r, r)
 
-    def s_copy(r):
-        return c_copy(ssend.at[r], srecv.at[c], s_s, s_r, r)
+    def s_copy(m):
+        return row_copy(ssend.at[m], srecv.at[c // 2], s_s, s_r, m)
 
     pages_dev = ctx_dev // PAGE
     page_row = lax.broadcasted_iota(jnp.int32, (2 * pages_dev, ctx_dev), 0)
@@ -171,31 +187,36 @@
     own_q.start()
     repeat(1, g, lambda r: z_copy(r).start())
     k_copy().start()
+    e_copy().start()
     first = max(2, n * 3 // 4)
     repeat(1, first, lambda r: q_copy(r).start())
     own_z.wait()
     repeat(1, g, lambda r: z_copy(r).wait_recv())
     own_i = pltpu.make_async_copy(zed, idx.at[0], loc.at[3])
     own_i.start()
-    repeat(1, n, lambda r: i_copy(r).start())
+    repeat(1, chips, lambda m: i_copy(m).start())
     repeat(first, n, lambda r: q_copy(r).start())
 
     def index_rows():
         own_i.wait()
-        repeat(1, n, lambda r: i_copy(r).wait_recv())
+        own_e.wait()
+        e_copy().wait_recv()
+        repeat(1, chips, lambda m: i_copy(m).wait_recv())
         count = g * hb
+        steps = ctx_dev // ichunk
 
         def lay(r):
             rows = idx[r]
             flat_query[r] = rows[:, 0].reshape(count, D_IDX)
             wide_gains[r] = rows[:, 1].reshape(count, D_IDX).astype(jnp.float32)
 
-        repeat(0, n, lay)
+        repeat(0, chips, lay)
 
         def block(s, carry):
             at = pl.ds(pl.multiple_of(s * ichunk, ichunk), ichunk)
-            keys = keys_ref[at, :]
-            for b in range(n // 4):
+            part = pl.ds(pl.multiple_of((s % steps) * ichunk, ichunk), ichunk)
+            keys = keys_all[s // steps, part, :]
+            for b in range(chips // 4):
                 dots = lax.dot_general(
                     flat_query[4 * b : 4 * b + 4].reshape(4 * count, D_IDX), keys,
                     (((1,), (1,)), ((), ())), preferred_element_type=jnp.float32,
@@ -215,21 +236,20 @@
                     ssend[r, :, at] = jnp.concatenate(sums, axis=1)
             return carry
 
-        lax.fori_loop(0, ctx_dev // ichunk, block, 0)
-        repeat(1, n, lambda r: s_copy(r).start())
-
-    own_s = pltpu.make_async_copy(ssend.at[0], srecv.at[c], loc.at[4])
+        lax.fori_loop(0, 2 * steps, block, 0)
+        repeat(1, chips, lambda m: s_copy(m).start())
+
+    own_s = pltpu.make_async_copy(ssend.at[0], srecv.at[c // 2], loc.at[4])
 
     own_k.wait()
     own_q.wait()
     k_copy().wait_recv()
     per = ctx_dev // chunk
     scale = ((QK_NOPE + D_ROPE) ** -0.5) * LOG2E
-    m_rows = group * half
-
-    def rows_of(b):
+    def rows_of(start, group):
+        m_rows = group * half
         for j in range(group):
-            r = b * group + j
+            r = start + j
             if isinstance(r, int):
                 if r > 0:
                     q_copy(r).wait_recv()
@@ -242,11 +262,11 @@
         def part_one(s, peak):
             keys = pl.ds(pl.multiple_of((s % per) * chunk, chunk), chunk)
             dots = jnp.dot(
-                qr[pl.ds(b * group, group)].reshape(m_rows, qr.shape[2]),
+                qr[pl.ds(start, group)].reshape(m_rows, qr.shape[2]),
                 kt[s // per, :, keys],
                 preferred_element_type=jnp.float32,
             ) * scale
-            logits[s] = dots
+            logits[s, :m_rows] = dots
             for t in range(chunk // 128):
                 peak = jnp.maximum(peak, dots[:, t * 128 : (t + 1) * 128])
             return peak
@@ -255,14 +275,14 @@
             0, 2 * per, part_one, jnp.full((m_rows, 128), -jnp.inf, jnp.float32), unroll=unroll
         )
         top = jnp.max(peak, axis=1, keepdims=True)
-        acc[...] = jnp.zeros_like(acc)
+        acc[:m_rows] = jnp.zeros((m_rows, D_LAT), jnp.float32)
 
         def part_two(s, total):
             keys = pl.ds(pl.multiple_of((s % per) * chunk, chunk), chunk)
-            expo = jnp.exp2(logits[s] - top)
+            expo = jnp.exp2(logits[s, :m_rows] - top)
             for t in range(chunk // 128):
                 total = total + expo[:, t * 128 : (t + 1) * 128]
-            acc[...] += lax.dot_general(
+            acc[:m_rows] += lax.dot_general(
                 expo.astype(jnp.bfloat16), kt[s // per, :D_LAT, keys],
                 (((1,), (1,)), ((), ())), preferred_element_type=jnp.float32,
             )
@@ -272,14 +292,14 @@
         mass = jnp.sum(total, axis=1, keepdims=True)
         lane = lax.broadcasted_iota(jnp.int32, (m_rows, 128), 1)
         stats = jnp.where(lane == 0, top, mass)
-        osend[pl.ds(b * group, group)] = acc[...].astype(jnp.bfloat16).reshape(
+        osend[pl.ds(start, group)] = acc[:m_rows].astype(jnp.bfloat16).reshape(
             group, half, D_LAT
         )
         for j in range(group):
             turned = jnp.transpose(stats[j * half : (j + 1) * half, :])
-            tsend[b * group + j] = jnp.concatenate([turned[:8], turned[:8]], axis=1)
+            tsend[start + j] = jnp.concatenate([turned[:8], turned[:8]], axis=1)
         for j in range(group):
-            r = b * group + j
+            r = start + j
             if isinstance(r, int):
                 if r > 0:
                     t_copy(r).start()
@@ -291,18 +311,23 @@
                     t_copy(r).start()
                     o_copy(r).start()
 
-    rows_of(0)
-    index_rows()
-    own_s.start()
-    repeat(1, n // group, rows_of)
+    plan = [(0, 4), (4, 2), (6, 2), None]
+    for piece in plan:
+        if piece is None:
+            index_rows()
+            own_s.start()
+        else:
+            rows_of(*piece)
+    if n > 8:
+        repeat(2, n // group, lambda b: rows_of(b * group, group))
 
     own_s.wait()
 
-    def take_scores(r):
-        peer = flip(c, r, n)
-        c_copy(ssend.at[r], srecv.at[peer], s_s, s_r, r).wait_recv()
-
-    repeat(1, n, take_scores)
+    def take_scores(m):
+        peer = flip(c // 2, m, chips)
+        row_copy(ssend.at[m], srecv.at[peer], s_s, s_r, m).wait_recv()
+
+    repeat(1, chips, take_scores)
     table = srecv[...]
     row_max = jnp.max(table)
     row_total = jnp.sum(jnp.exp(table - row_max), keepdims=True)
@@ -339,15 +364,20 @@
 
     repeat(1, g, lambda r: z_copy(r).wait_send())
     k_copy().wait_send()
+    e_copy().wait_send()
 
     def sent(r):
         q_copy(r).wait_send()
-        i_copy(r).wait_send()
         o_copy(r).wait_send()
         t_copy(r).wait_send()
-        s_copy(r).wait_send()
 
     repeat(1, n, sent)
+
+    def sent_rows(m):
+        i_copy(m).wait_send()
+        s_copy(m).wait_send()
+
+    repeat(1, chips, sent_rows)
 
 
 def per_device(n, g, idx_query, idx_weight, idx_keys, q_latent, latent_cache, page_ids):
@@ -359,24 +389,26 @@
     full = width + 2 * pages_dev
     half = H // 2
     dma = pltpu.SemaphoreType.DMA
+    anywhere = pl.BlockSpec(memory_space=pl.ANY)
     vmem = pl.BlockSpec(memory_space=pltpu.VMEM)
     logp, out = pl.pallas_call(
         functools.partial(kernel, n, g, group, chunk, ichunk, unroll),
         out_shape=(
-            jax.ShapeDtypeStruct((n, 1, ctx_dev), jnp.float32),
+            jax.ShapeDtypeStruct((chips, 1, 2 * ctx_dev), jnp.float32),
             jax.ShapeDtypeStruct((half, 2 * D_LAT), jnp.bfloat16),
         ),
-        in_specs=[vmem, vmem, pl.BlockSpec(memory_space=pl.ANY), vmem, vmem, vmem],
+        in_specs=[vmem, vmem, anywhere, anywhere, vmem, vmem],
         out_specs=(vmem, vmem),
         scratch_shapes=[
             pltpu.VMEM((g, hb, D_IDX), jnp.float32),
             pltpu.VMEM((g, 2, hb, D_IDX), jnp.bfloat16),
             pltpu.VMEM((half, 2 * width), jnp.float32),
             pltpu.VMEM((chips, 2, half, full), jnp.bfloat16),
-            pltpu.VMEM((n, g * hb, D_IDX), jnp.bfloat16),
-            pltpu.VMEM((n, g * hb, D_IDX), jnp.float32),
+            pltpu.VMEM((chips, g * hb, D_IDX), jnp.bfloat16),
+            pltpu.VMEM((chips, g * hb, D_IDX), jnp.float32),
             pltpu.VMEM((g, 2, hb, D_IDX), jnp.bfloat16),
-            pltpu.VMEM((n, g, 2, hb, D_IDX), jnp.bfloat16),
+            pltpu.VMEM((chips, g, 2, hb, D_IDX), jnp.bfloat16),
+            pltpu.VMEM((2, ctx_dev, D_IDX), jnp.bfloat16),
             pltpu.VMEM((2, full, ctx_dev), jnp.bfloat16),
             pltpu.VMEM((n, half, full), jnp.bfloat16),
             pltpu.VMEM((2 * ctx_dev // chunk, group * half, chunk), jnp.float32),
@@ -385,8 +417,8 @@
             pltpu.VMEM((n, half, D_LAT), jnp.bfloat16),
             pltpu.VMEM((n, 8, 128), jnp.float32),
             pltpu.VMEM((n, 8, 128), jnp.float32),
-            pltpu.VMEM((n, 1, ctx_dev), jnp.float32),
-            pltpu.VMEM((n, 1, ctx_dev), jnp.float32),
+            pltpu.VMEM((chips, 1, 2 * ctx_dev), jnp.float32),
+            pltpu.VMEM((chips, 1, 2 * ctx_dev), jnp.float32),
             dma((g,)), dma((g,)),
             dma((n,)), dma((n,)),
             dma, dma,
@@ -394,7 +426,8 @@
             dma((n,)), dma((n,)),
             dma((n,)), dma((n,)),
             dma((n,)), dma((n,)),
-            dma((5,)),
+            dma, dma,
+            dma((6,)),
         ],
         compiler_params=pltpu.CompilerParams(
             collective_id=0, has_side_effects=True, vmem_limit_bytes=60 * 1024 * 1024

time: 35.9 us -> 34.2 us (0.953)
  Pallas kernels: 31.8 us -> 30.1 us
    pallas_call x1, Pallas kernels: 31.8 us -> 30.1 us  [per_device(): pl.pallas_call(functools.partial(kernel, n, g, group, chunk, ichunk, unro...]
where the time goes in v3:
time: 34.2 us; the launch traced here: 34 us
  Pallas kernels  30.1 us (88%)
  local copies, waits for them, and re-layouts  3.28 us (10%)
  between operations  0.64 us (2%)
    pallas_call x1, Pallas kernels, per_device(): pl.pallas_call(functools.partial(kernel, n, g, group, chunk, ichunk, unro...  30.1 us
    unnamed x2, local copies, waits for them, and re-layouts  3.28 us

profile of v3, /device:TPU:0, one launch (start us, length us, event | category | flops | bytes accessed | tf_op | source)
XLA Modules:
  0.0 34.0 jit_solution(9073737516385799489)
XLA Ops:
  0.6 30.1 %shard_map.77 = (f32[4,1,4096]{2,1,0:T(1,128)}, bf16[64,1024]{1,0:T(8,128)(2,1)}) custom-call(bf16[4,2048]{1,0:T(4,128)(2,1)} %heads_ref.1, bf16[4,16]{1,0:T(4,128)(2,1)} %gains_ref.1, bf16[576,2048]{1,0:T(8,128)(2,1)} %bitcast.5, bf16[2048,128]{1,0:T(8,128)(2,1)} %keys_ref.1, bf16[1,73728]{1,0:T(2,128)(2,1)} %latent_ref.1, s32[1,32]{1,0:T(1,128)} %pages_ref.1), custom_call_target="tpu_custom_call" | custom-call | tf_op jit(solution)/shard_map/pallas_call | solution.py:394
  30.7 1.8 %copy.8 = bf16[1,1,64,1024]{3,1,2,0:T(2,128)(2,1)} copy(bf16[1,1,64,1024]{3,2,1,0:T(8,128)(2,1)} %bitcast.7) | data formatting | bytes 262144
  32.5 1.5 %copy.10 = f32[1,16384]{1,0:T(1,128)} copy(f32[1,16384]{1,0:T(1,128)} %bitcast.8) | data formatting | bytes 131072
